TPU v7x, 32 devices: a whole 2x2x4 slice. The times are simulated.
32 devices in a mesh: parts: 2 (over y), seq: 8 (over z, core), rep: 2 (over x), head: 1.
Axes of the slice: x: 2, y: 2, z: 4, core: 2. Of those that a mesh axis runs over, the one named last changes fastest.
Arguments:
- activations: bfloat16 [4, 1024, 2048], P(('parts', 'rep'), 'seq', 'head'), parts along dimension 0, may hold values from -6 to 6
- value_weight: bfloat16 [2048, 2048], P(('seq', 'rep'), 'head'), may hold values from -0.125 to 0.125
- query_in: bfloat16 [4, 1024, 2048], P(('parts', 'rep'), 'seq', 'head'), parts along dimension 0, may hold values from -6 to 6
- key_in: bfloat16 [4, 1024, 2048], P(('parts', 'rep'), 'seq', 'head'), parts along dimension 0, may hold values from -6 to 6
- grad_out: bfloat16 [4, 1024, 2048], P(('parts', 'rep'), 'seq', 'head'), parts along dimension 0, may hold values from -6 to 6
- conv_kernel: float32 [3, 4, 2048], P(None, None, 'head'), may hold values from -3 to 3
- log_gate: float32 [4, 16, 1024], P(('parts', 'rep'), 'head', 'seq'), parts along dimension 0, as said below
Outputs:
- attn_out: bfloat16 [4, 1024, 2048], P(('parts', 'rep'), 'seq', 'head'), parts along dimension 0
- grad_query: bfloat16 [4, 1024, 2048], P(('parts', 'rep'), 'seq', 'head'), parts along dimension 0
- grad_key: bfloat16 [4, 1024, 2048], P(('parts', 'rep'), 'seq', 'head'), parts along dimension 0
- grad_x: bfloat16 [4, 1024, 2048], P(('parts', 'rep'), 'seq', 'head'), parts along dimension 0
- grad_w: float32 [4096, 2048], P(('parts', 'seq', 'rep'), 'head'), parts along dimension 0
- grad_conv: float32 [6, 4, 2048], P('parts', None, 'head'), parts along dimension 0
There are 2 independent parts, one for each index of `parts`. A program takes and returns all parts, laid end to end along the dimension named above; an argument that names none is the same for every part. Nothing has to cross between parts.
Inputs may be any that keep to these rules, and one draw needn't show every extreme that they name: `log_gate`: every entry is below zero.
All inputs are finite; a program needn't handle non-finite values.
Results may differ from a plain program's by a relative error of at most 0.015.
Values may be sent and summed in bfloat16 or wider, within the bound.
A program may use at most 128 MiB of HBM per device.

v0:
```python
import math
import jax
import jax.numpy as jnp
from jax import lax
from jax.sharding import PartitionSpec as P

EPSILON = 1e-06


def shifted(block, axis, distance):
    devices = range(lax.axis_size(axis))
    route = [(i - distance, i) for i in devices if i - distance in devices]
    return lax.ppermute(block, axis, route)


def prefix(part, axis, combine, identity, reverse):
    count = lax.axis_size(axis)
    place = lax.axis_index(axis)
    ahead = count - 1 - place if reverse else place
    gathered = jax.tree.map(lambda a: lax.all_gather(a, axis), part)
    state = jax.tree.map(lambda a, e: jnp.zeros_like(a) + jnp.asarray(e, a.dtype), part, identity)

    def one(step, state):
        source = count - 1 - step if reverse else step
        return combine(
            state, jax.tree.map(lambda a: lax.dynamic_index_in_dim(a, source, 0, False), gathered)
        )

    return lax.fori_loop(0, ahead, one, state)


def carried_in(value, axis, combine, identity, reverse):
    length, mine = (lax.axis_size(axis), lax.axis_index(axis))
    everything = jax.tree.map(
        lambda part, kind: lax.all_gather(part.astype(kind), axis),
        value,
        (jnp.bfloat16, jnp.bfloat16),
    )
    start = jax.tree.map(
        lambda part, zero: jnp.broadcast_to(jnp.asarray(zero, part.dtype), part.shape),
        value,
        identity,
    )

    def step(k, before):
        at = length - 1 - k if reverse else k
        reached = at > mine if reverse else at < mine
        new = combine(
            before, jax.tree.map(lambda part, own: part[at].astype(own.dtype), everything, value)
        )
        return jax.tree.map(lambda a, b: jnp.where(reached, a, b), new, before)

    return lax.fori_loop(0, length, step, start)


def chain_join(earlier, following):
    return (earlier[0] * following[0], following[0][:, None, None] * earlier[1] + following[1])


def causal_filter(stream_rows, previous, kernel_taps):
    rim_rows = previous.shape[0]
    length = stream_rows.shape[0]
    extended = jnp.concatenate([previous, stream_rows], axis=0).astype(jnp.float32)
    result = jnp.zeros(stream_rows.shape, jnp.float32)
    for offset in range(kernel_taps.shape[0]):
        result = (
            result + kernel_taps[offset] * extended[rim_rows - offset : rim_rows - offset + length]
        )
    return result


def filter_back(post_rows, following_rows, kernel_taps):
    length = post_rows.shape[0]
    extended = jnp.concatenate([post_rows, following_rows], axis=0)
    result = jnp.zeros(post_rows.shape, jnp.float32)
    for offset in range(kernel_taps.shape[0]):
        result = result + kernel_taps[offset] * extended[offset : offset + length]
    return result


def tap_sums(post_rows, stream_rows, previous, kernel_width):
    rim_rows = previous.shape[0]
    length = stream_rows.shape[0]
    extended = jnp.concatenate([previous, stream_rows], axis=0).astype(jnp.float32)
    return jnp.stack(
        [
            jnp.sum(post_rows * extended[rim_rows - offset : rim_rows - offset + length], axis=0)
            for offset in range(kernel_width)
        ]
    )


def local(activations, value_weight, query_in, key_in, grad_out, conv_kernel, log_gate):
    tok_rows = query_in.shape[1]
    channels = query_in.shape[2]
    head_count = log_gate.shape[1]
    head_size = channels // head_count
    kernel_width = conv_kernel.shape[1]
    rim_rows = kernel_width - 1
    grad_scale = 1.0 / math.sqrt(lax.axis_size("seq") * lax.axis_size("rep") * tok_rows)
    query_rows = query_in[0]
    key_rows = key_in[0]
    gathered = lax.all_gather(activations, "head", axis=2, tiled=True)[0]
    columns = gathered
    value_f32 = jnp.dot(
        columns,
        lax.all_gather(value_weight, ("seq", "rep"), axis=0, tiled=True),
        preferred_element_type=jnp.float32,
    )
    value_raw = value_f32.astype(jnp.bfloat16)
    before_all = shifted(
        jnp.stack(
            [
                query_rows[tok_rows - rim_rows :],
                key_rows[tok_rows - rim_rows :],
                value_raw[tok_rows - rim_rows :],
            ]
        ),
        "seq",
        1,
    )
    before = (before_all[0], before_all[1], before_all[2])
    raw_rows = (query_rows, key_rows, value_raw)
    convolved = [
        causal_filter(raw_rows[which], before[which], conv_kernel[which]).astype(jnp.bfloat16)
        for which in range(3)
    ]
    query_heads = convolved[0].reshape(tok_rows, head_count, head_size)
    key_heads = convolved[1].reshape(tok_rows, head_count, head_size)
    value_heads = convolved[2].reshape(tok_rows, head_count, head_size)
    cumulative = jnp.cumsum(log_gate[0], axis=1)
    final_cum = cumulative[:, -1]
    block_decay = jnp.exp(final_cum)
    rising = jnp.exp(cumulative).T[:, :, None]
    shrink = jnp.exp(final_cum[:, None] - cumulative).T[:, :, None]
    mixing = jnp.exp(-jnp.abs(cumulative[:, :, None] - cumulative[:, None, :]))
    scores = (
        mixing
        * jnp.einsum("thd,shd->hts", query_heads, key_heads, preferred_element_type=jnp.float32)
    ).astype(jnp.bfloat16)
    fwd_sum = jnp.einsum(
        "thd,the->hde",
        (shrink * key_heads).astype(jnp.bfloat16),
        value_heads,
        preferred_element_type=jnp.float32,
    )
    back_sum = jnp.einsum(
        "thd,the->hde",
        (rising * key_heads).astype(jnp.bfloat16),
        value_heads,
        preferred_element_type=jnp.float32,
    )
    identity = (
        jnp.ones((head_count,), jnp.float32),
        jnp.zeros((head_count, head_size, head_size), jnp.float32),
    )
    left_b = prefix((block_decay, fwd_sum), "seq", chain_join, identity, False)[1].astype(
        jnp.bfloat16
    )
    right_b = prefix((block_decay, back_sum), "seq", chain_join, identity, True)[1].astype(
        jnp.bfloat16
    )
    attn = rising * jnp.einsum(
        "thd,hde->the", query_heads, left_b, preferred_element_type=jnp.float32
    )
    attn = attn + shrink * jnp.einsum(
        "thd,hde->the", query_heads, right_b, preferred_element_type=jnp.float32
    )
    attn = attn + jnp.einsum(
        "hts,she->the", scores, value_heads, preferred_element_type=jnp.float32
    )
    root_mean = jnp.sqrt(jnp.mean(attn * attn, axis=2, keepdims=True) + EPSILON)
    normed = attn / root_mean
    attn_out = normed.astype(jnp.bfloat16).reshape(1, tok_rows, channels)
    upstream = grad_out[0].reshape(tok_rows, head_count, head_size).astype(jnp.float32)
    grad_attn = (
        (upstream - normed * jnp.mean(upstream * normed, axis=2, keepdims=True)) / root_mean
    ).astype(jnp.bfloat16)
    grad_scores = (
        mixing
        * jnp.einsum("the,she->hts", grad_attn, value_heads, preferred_element_type=jnp.float32)
    ).astype(jnp.bfloat16)
    fwd_grad = jnp.einsum(
        "thd,the->hde",
        (shrink * query_heads).astype(jnp.bfloat16),
        grad_attn,
        preferred_element_type=jnp.float32,
    )
    back_grad = jnp.einsum(
        "thd,the->hde",
        (rising * query_heads).astype(jnp.bfloat16),
        grad_attn,
        preferred_element_type=jnp.float32,
    )
    left_gb = carried_in((block_decay, fwd_grad), "seq", chain_join, identity, False)[1].astype(
        jnp.bfloat16
    )
    right_gb = carried_in((block_decay, back_grad), "seq", chain_join, identity, True)[1].astype(
        jnp.bfloat16
    )
    query_post = rising * jnp.einsum(
        "the,hde->thd", grad_attn, left_b, preferred_element_type=jnp.float32
    )
    query_post = query_post + shrink * jnp.einsum(
        "the,hde->thd", grad_attn, right_b, preferred_element_type=jnp.float32
    )
    query_post = query_post + jnp.einsum(
        "hts,shd->thd", grad_scores, key_heads, preferred_element_type=jnp.float32
    )
    key_post = rising * jnp.einsum(
        "the,hde->thd", value_heads, left_gb, preferred_element_type=jnp.float32
    )
    key_post = key_post + shrink * jnp.einsum(
        "the,hde->thd", value_heads, right_gb, preferred_element_type=jnp.float32
    )
    key_post = key_post + jnp.einsum(
        "hts,thd->shd", grad_scores, query_heads, preferred_element_type=jnp.float32
    )
    value_post = rising * jnp.einsum(
        "thd,hde->the", key_heads, left_gb, preferred_element_type=jnp.float32
    )
    value_post = value_post + shrink * jnp.einsum(
        "thd,hde->the", key_heads, right_gb, preferred_element_type=jnp.float32
    )
    value_post = value_post + jnp.einsum(
        "hts,the->she", scores, grad_attn, preferred_element_type=jnp.float32
    )
    post_grads = jnp.stack(
        [
            query_post.reshape(tok_rows, channels),
            key_post.reshape(tok_rows, channels),
            value_post.reshape(tok_rows, channels),
        ]
    )
    following = shifted(post_grads[:, :rim_rows].astype(jnp.bfloat16), "seq", -1).astype(
        jnp.float32
    )
    grad_query = filter_back(post_grads[0], following[0], conv_kernel[0]).astype(jnp.bfloat16)
    grad_key = filter_back(post_grads[1], following[1], conv_kernel[1]).astype(jnp.bfloat16)
    grad_value = filter_back(post_grads[2], following[2], conv_kernel[2]).astype(jnp.bfloat16)
    kernel_terms = (
        jnp.stack(
            [
                tap_sums(post_grads[which], raw_rows[which], before[which], kernel_width)
                for which in range(3)
            ]
        )
        * grad_scale
    )
    grad_conv = lax.psum(kernel_terms, ("seq", "rep"))
    partial_x = lax.dot_general(
        grad_value,
        lax.all_gather(value_weight, ("seq", "rep"), axis=0, tiled=True),
        (((1,), (1,)), ((), ())),
        preferred_element_type=jnp.float32,
    )
    grad_x = lax.psum_scatter(
        partial_x[None].astype(jnp.bfloat16), "head", scatter_dimension=2, tiled=True
    )
    columns = gathered
    grad_w = lax.psum_scatter(
        lax.dot_general(
            columns, grad_value, (((0,), (0,)), ((), ())), preferred_element_type=jnp.float32
        )
        * grad_scale,
        ("seq", "rep"),
        scatter_dimension=0,
        tiled=True,
    )
    return (attn_out, grad_query[None], grad_key[None], grad_x, grad_w, grad_conv)


def solution(mesh):
    placed = (
        P(("parts", "rep"), "seq", "head"),
        P(("seq", "rep"), "head"),
        P(("parts", "rep"), "seq", "head"),
        P(("parts", "rep"), "seq", "head"),
        P(("parts", "rep"), "seq", "head"),
        P(None, None, "head"),
        P(("parts", "rep"), "head", "seq"),
    )
    return jax.shard_map(
        local,
        mesh=mesh,
        in_specs=placed,
        out_specs=(
            P(("parts", "rep"), "seq", "head"),
            P(("parts", "rep"), "seq", "head"),
            P(("parts", "rep"), "seq", "head"),
            P(("parts", "rep"), "seq", "head"),
            P(("parts", "seq", "rep"), "head"),
            P("parts", None, "head"),
        ),
        check_vma=False,
    )
```

profile of v0, /device:TPU:0, one launch (start us, length us, event | category | flops | bytes accessed | tf_op | source)
XLA Modules:
  0.0 710.2 jit_solution(15877381056896727067)
XLA Ops:
  11.9 75.4 %all-gather.12.cloned.1.call-done = bf16[2048,2048]{1,0:T(8,128)(2,1)} async-done(((bf16[128,2048]{1,0:T(8,128)(2,1)}), bf16[2048,2048]{1,0:T(8,128)(2,1)}) %all-gather.12.cloned.1.call-update) | async-done | bytes 8388624 | tf_op jit(solution)/shard_map/all_gather | solution.py:107
  87.2 4.6 convolution_convert_fusion.1
  99.2 2.3 fusion.54
  101.6 2.3 copy.108
  105.4 16.3 %all-reduce = f32[128]{0:T(128)S(1)} all-reduce(f32[128]{0:T(128)S(1)} %dynamic-update-slice), channel_id=2, replica_groups=mesh['parts'=2,'seq'=8,'rep'=2,'head'=1] {'seq'}, use_global_device_ids=true, to_apply=%add | all-reduce | flops 128 | bytes 1024
  125.5 2.4 fusion.19
  127.9 54.5 %all-gather.14.cloned.1.call-done = f32[128,128,128]{2,1,0:T(8,128)} async-done(((f32[16,128,128]{2,1,0:T(8,128)}), f32[128,128,128]{2,1,0:T(8,128)}) %all-gather.14.cloned.1.call-update) | async-done | bytes 8388624 | tf_op jit(solution)/shard_map/all_gather | solution.py:20
  183.5 2.6 fusion.18
  186.2 78.5 %all-gather.16.cloned.1.call-done = f32[128,128,128]{2,1,0:T(8,128)} async-done(((f32[16,128,128]{2,1,0:T(8,128)}), f32[128,128,128]{2,1,0:T(8,128)}) %all-gather.16.cloned.1.call-update) | async-done | bytes 8388624 | tf_op jit(solution)/shard_map/all_gather | solution.py:20
  265.8 18.6 %while.57 = (s32[]{:T(128)}, f32[16,128,128]{2,1,0:T(8,128)}, s32[]{:T(128)}, f32[8,16]{1,0:T(8,128)S(1)}, f32[8,16,128,128]{3,2,1,0:T(8,128)}, /*index=5*/s32[]{:T(128)}, s32[]{:T(128)}, s32[]{:T(128)}, s32[]{:T(128)}) while((s32[]{:T(128)}, f32[16,128,128]{2,1,0:T(8,128)}, s32[]{:T(128)}, f32[8,16]{1,0:T(8,128)S(1)}, ...), condition=%wide.region_4.5_spmd, body=%wide.region_3.4_spmd.sunk | while | flops 524294 | bytes 3146075 | solution.py:29
  265.8 2.7 bitcast_add_fusion.5
  268.4 2.7 bitcast_add_fusion.5
  271.1 2.7 bitcast_add_fusion.5
  273.8 2.7 bitcast_add_fusion.5
  276.4 2.7 bitcast_add_fusion.5
  279.1 2.7 bitcast_add_fusion.5
  281.7 2.7 bitcast_add_fusion.5
  291.0 2.3 convolution_convert_fusion.2
  293.9 14.5 %all-reduce.1 = bf16[128]{0:T(256)(128)(2,1)S(1)} all-reduce(bf16[128]{0:T(256)(128)(2,1)S(1)} %dynamic-update-slice.1), channel_id=7, replica_groups=mesh['parts'=2,'seq'=8,'rep'=2,'head'=1] {'seq'}, use_global_device_ids=true, to_apply=%add.1 | all-reduce | flops 128 | bytes 512
  316.6 19.6 %all-gather.18.cloned.1.call-done = bf16[128,128,128]{2,1,0:T(8,128)(2,1)} async-done(((bf16[16,128,128]{2,1,0:T(8,128)(2,1)}), bf16[128,128,128]{2,1,0:T(8,128)(2,1)}) %all-gather.18.cloned.1.call-update) | async-done | bytes 4194320 | tf_op jit(solution)/shard_map/all_gather | solution.py:35
  336.2 20.2 %while.58 = (s32[]{:T(128)}, f32[16,128,128]{2,1,0:T(8,128)}, s32[]{:T(128)}, bf16[8,16]{1,0:T(8,128)(2,1)S(1)}, bf16[8,16,128,128]{3,2,1,0:T(8,128)(2,1)}, /*index=5*/s32[]{:T(128)}, s32[]{:T(128)}) while((s32[]{:T(128)}, f32[16,128,128]{2,1,0:T(8,128)}, s32[]{:T(128)}, bf16[8,16]{1,0:T(8,128)(2,1)S(1)}, ...), condition=%wide.region_8.9_spmd.clone, body=%wide.region_7.8_spmd.clone.sunk | while | flops 1310740 | bytes 2621713 | solution.py:53
  338.5 2.5 fusion.119
  341.0 2.5 fusion.119
  343.6 2.6 fusion.119
  346.2 2.5 fusion.119
  348.8 2.5 fusion.119
  351.3 2.6 fusion.119
  353.9 2.5 fusion.119
  356.4 2.8 fusion.6
  360.7 22.6 %all-gather.20.cloned.1.call-done = bf16[128,128,128]{2,1,0:T(8,128)(2,1)} async-done(((bf16[16,128,128]{2,1,0:T(8,128)(2,1)}), bf16[128,128,128]{2,1,0:T(8,128)(2,1)}) %all-gather.20.cloned.1.call-update) | async-done | bytes 4194320 | tf_op jit(solution)/shard_map/all_gather | solution.py:35
  383.4 20.9 %while.59 = (s32[]{:T(128)}, f32[16,128,128]{2,1,0:T(8,128)}, s32[]{:T(128)}, bf16[8,16]{1,0:T(8,128)(2,1)S(1)}, bf16[8,16,128,128]{3,2,1,0:T(8,128)(2,1)}, /*index=5*/s32[]{:T(128)}, s32[]{:T(128)}, s32[]{:T(128)}, s32[]{:T(128)}) while((s32[]{:T(128)}, f32[16,128,128]{2,1,0:T(8,128)}, s32[]{:T(128)}, ...), condition=%wide.region_10.11_spmd.clone, body=%wide.region_9.10_spmd.clone.sunk | while | flops 1310744 | bytes 2621775 | solution.py:53
  383.4 2.3 fusion.120
  385.7 2.6 fusion.120
  388.3 2.6 fusion.120
  391.0 2.6 fusion.120
  393.6 2.6 fusion.120
  396.3 2.6 fusion.120
  398.9 2.6 fusion.120
  401.6 2.6 fusion.120
  417.7 2.5 copy.157
  420.3 3.6 multiply_reduce_fusion.3
  423.9 8.1 %multiply_bitcast_fusion = f32[2048,2048]{0,1:T(8,128)} fusion(bf16[128,2048]{1,0:T(8,128)(2,1)S(1)} %get-tuple-element.476, bf16[1,128,2048]{2,1,0:T(8,128)(2,1)S(1)} %copy-done), kind=kOutput, calls=%fused_computation.10 | convolution fusion | flops 1077936128 | bytes 17825792 | tf_op jit(solution)/shard_map/dot_general | solution.py:262
  435.7 2.5 copy.126
  438.3 4.3 multiply_reduce_fusion.7
  445.1 8.5 %fusion.2 = bf16[1,128,2048]{2,1,0:T(8,128)(2,1)} fusion(bf16[128,2048]{1,0:T(8,128)(2,1)S(1)} %get-tuple-element.476, bf16[2048,2048]{1,0:T(8,128)(2,1)} %all-gather.12.cloned.1.call-done), kind=kOutput, calls=%fused_computation.13 | convolution fusion | flops 1074003968 | bytes 9437184 | tf_op jit(solution)/shard_map/dot_general | solution.py:251
  453.6 156.4 %reduce-scatter.2.cloned.1.call-done = f32[128,2048]{0,1:T(8,128)} async-done(((f32[2048,2048]{0,1:T(8,128)}), f32[128,2048]{0,1:T(8,128)}) %reduce-scatter.2.cloned.1.call-update) | async-done | bytes 1048592 | tf_op jit(solution)/shard_map/reduce_scatter | solution.py:261
  610.0 2.5 copy.138
  612.5 89.3 %all-reduce.4.cloned.1.call-done = f32[3,4,2048]{2,1,0:T(4,128)} async-done(((f32[3,4,2048]{2,1,0:T(4,128)}), f32[3,4,2048]{2,1,0:T(4,128)}) %all-reduce.4.cloned.1.call-update) | async-done | bytes 98320 | tf_op jit(solution)/shard_map/psum | solution.py:250
  (152 shorter events, 59.2 us)
Async XLA Ops:
  7.2 80.1 %copy-start = (bf16[1,128,2048]{2,1,0:T(8,128)(2,1)S(1)}, bf16[1,128,2048]{2,1,0:T(8,128)(2,1)}, u32[]{:S(2)}) copy-start(bf16[1,128,2048]{2,1,0:T(8,128)(2,1)} %param.15) | copy-start | bytes 1572868
  7.2 80.1 %all-gather.12.cloned.1.call-start = ((), (), s32[]{:S(2)}) async-start(), calls=%async_computation.1 | async-start | bytes 8912896 | tf_op jit(solution)/shard_map/all_gather | solution.py:107
  7.9 174.5 %all-gather.14.cloned.1.call-start = ((), (), s32[]{:S(2)}) async-start(), calls=%async_computation.4 | async-start | bytes 9437184 | tf_op jit(solution)/shard_map/all_gather | solution.py:20
  11.9 83.1 %copy-start.22 = (bf16[1,128,2048]{2,1,0:T(8,128)(2,1)S(1)}, bf16[1,128,2048]{2,1,0:T(8,128)(2,1)}, u32[]{:S(2)}) copy-start(bf16[1,128,2048]{2,1,0:T(8,128)(2,1)} %param.18) | copy-start | bytes 1572868
  92.0 3.0 collective-permute-start
  96.8 1.0 copy-start.12
  97.3 1.9 copy-start.9
  99.2 165.5 %all-gather.16.cloned.1.call-start = ((), (), s32[]{:S(2)}) async-start(), calls=%async_computation.5 | async-start | bytes 9437184 | tf_op jit(solution)/shard_map/all_gather | solution.py:20
  101.5 2.4 copy-start.24
  101.5 20.2 %copy-start.23 = (bf16[1,128,2048]{2,1,0:T(8,128)(2,1)S(1)}, bf16[1,128,2048]{2,1,0:T(8,128)(2,1)}, u32[]{:S(2)}) copy-start(bf16[1,128,2048]{2,1,0:T(8,128)(2,1)} %param.17) | copy-start | bytes 1572868
  101.6 234.7 %all-gather.18.cloned.1.call-start = ((), (), s32[]{:S(2)}) async-start(), calls=%async_computation.6 | async-start | bytes 4718592 | tf_op jit(solution)/shard_map/all_gather | solution.py:35
  121.9 1.1 copy-start.1
  284.4 2.0 copy-start.10
  284.4 2.0 copy-start.20
  286.4 1.2 copy-start.14
  288.8 0.8 copy-start.6
  290.9 92.4 %all-gather.20.cloned.1.call-start = ((), (), s32[]{:S(2)}) async-start(), calls=%async_computation.7 | async-start | bytes 4718592 | tf_op jit(solution)/shard_map/all_gather | solution.py:35
  293.3 316.7 %reduce-scatter.2.cloned.1.call-start = ((), (), s32[]{:S(2)}) async-start(), calls=%async_computation.2 | async-start | bytes 17825792 | tf_op jit(solution)/shard_map/reduce_scatter | solution.py:261
  308.5 1.9 copy-start.4
  308.5 1.9 copy-start.7
  310.4 1.7 copy-start.17
  310.4 1.4 copy-start.3
  311.9 1.0 copy-start.13
  356.4 2.8 copy-start.5
  356.4 2.8 copy-start.11
  404.2 2.1 copy-start.8
  404.2 2.2 copy-start.21
  409.9 2.2 copy-start.18
  413.5 2.1 copy-start.19
  416.4 3.9 collective-permute-start.1
  432.0 2.4 copy-start.15
  432.0 269.8 %all-reduce.4.cloned.1.call-start = ((), (), s32[]{:S(2)}) async-start(), calls=%async_computation.3 | async-start | bytes 196608 | tf_op jit(solution)/shard_map/psum | solution.py:250
  438.3 4.3 copy-start.2
  438.3 4.3 copy-start.16
Sparse Core Ops, SparseCore 0:
  10.2 76.9 all-gather.11
  99.3 83.1 all-gather.13
  184.1 80.5 all-gather.15
  291.1 45.1 all-gather.17
  337.7 45.6 all-gather.19
  432.1 177.8 reduce-scatter.1
  614.0 87.7 all-reduce.3
where the time goes:
time: 712 us; the launch traced here: 710 us
  waiting for transfers between devices  498 us (70%)
  other arithmetic  75.9 us (11%)
  matrix products  51.7 us (7%)
  local copies, waits for them, and re-layouts  34.8 us (5%)
  blocking collectives  30.8 us (4%)
  between operations  15.2 us (2%)
    reduce_scatter x1, waiting for transfers between devices, local(): lax.psum_scatter(lax.dot_general(columns, grad_value, (((0,), (0,)), ((),...  156 us
    all_gather x2, waiting for transfers between devices, prefix(): gathered = jax.tree.map(lambda a: lax.all_gather(a, axis), part)  133 us
    psum x1, waiting for transfers between devices, local(): grad_conv = lax.psum(kernel_terms, ('seq', 'rep'))  89.3 us
    all_gather x1, waiting for transfers between devices, local(): lax.all_gather(value_weight, ('seq', 'rep'), axis=0, tiled=True)  75.4 us
    all_gather x2, waiting for transfers between devices, carried_in(): lax.all_gather(part.astype(kind), axis)  42.3 us
    select_n x16, other arithmetic, step(): return jax.tree.map(lambda a, b: jnp.where(reached, a, b), new, before)  40.9 us
    unnamed x2, blocking collectives  30.8 us
    add x7, other arithmetic, chain_join(): following[0][:, None, None] * earlier[1] + following[1]  18.6 us
  transfers between devices with their start and end apart: 9, of which 8 were waited for; matrix products, arithmetic and copies ran while one was open for 11% of the time, Pallas kernels for 0%

commit v1 on v0

--- a/solution.py
+++ b/solution.py
@@ -104,7 +104,12 @@
     columns = gathered
     value_f32 = jnp.dot(
         columns,
-        lax.all_gather(value_weight, ("seq", "rep"), axis=0, tiled=True),
+        jnp.concatenate(
+            lax.all_to_all(
+                jnp.stack([value_weight] * lax.axis_size(("seq", "rep"))), ("seq", "rep"), 0, 0
+            ),
+            axis=0,
+        ),
         preferred_element_type=jnp.float32,
     )
     value_raw = value_f32.astype(jnp.bfloat16)

time: 712 us -> 858 us (1.21)
  waiting for transfers between devices: 498 us -> 601 us
  blocking collectives: 30.8 us -> 52.5 us
  starting transfers between devices: 3.96 us -> 22.3 us
    all_to_all x0 -> x1, waiting for transfers between devices: none -> 150 us  [local(): lax.all_to_all(jnp.stack([value_weight] * lax.axis_size(('seq', 'rep'))),...]
    all_gather x1, waiting for transfers between devices: 75.4 us -> 11.6 us  [local(): lax.all_gather(value_weight, ('seq', 'rep'), axis=0, tiled=True)]
    unnamed x2, blocking collectives: 30.8 us -> 52.5 us
    reduce_scatter x1, waiting for transfers between devices: 156 us -> 173 us  [local(): lax.psum_scatter(lax.dot_general(columns, grad_value, (((0,), (0,)), ((),...]
    ppermute x2, starting transfers between devices: 3.45 us -> 14.3 us  [shifted(): return lax.ppermute(block, axis, route)]
  transfers between devices with their start and end apart: 9 -> 10, of which waited for: 8 -> 9; matrix products, arithmetic and copies ran while one was open for 11% -> 14% of each run, Pallas kernels for 0% -> 0%
where the time goes in v1:
time: 858 us; the launch traced here: 856 us
  waiting for transfers between devices  601 us (70%)
  other arithmetic  76.1 us (9%)
  blocking collectives  52.5 us (6%)
  matrix products  48.6 us (6%)
  local copies, waits for them, and re-layouts  40.7 us (5%)
  starting transfers between devices  22.3 us (3%)
  between operations  15.2 us (2%)
    reduce_scatter x1, waiting for transfers between devices, local(): lax.psum_scatter(lax.dot_general(columns, grad_value, (((0,), (0,)), ((),...  173 us
    all_to_all x1, waiting for transfers between devices, local(): lax.all_to_all(jnp.stack([value_weight] * lax.axis_size(('seq', 'rep'))),...  150 us
    all_gather x2, waiting for transfers between devices, prefix(): gathered = jax.tree.map(lambda a: lax.all_gather(a, axis), part)  132 us
    psum x1, waiting for transfers between devices, local(): grad_conv = lax.psum(kernel_terms, ('seq', 'rep'))  89.3 us
    unnamed x2, blocking collectives  52.5 us
    all_gather x2, waiting for transfers between devices, carried_in(): lax.all_gather(part.astype(kind), axis)  43.4 us
    select_n x16, other arithmetic, step(): return jax.tree.map(lambda a, b: jnp.where(reached, a, b), new, before)  40.7 us
    add x7, other arithmetic, chain_join(): following[0][:, None, None] * earlier[1] + following[1]  18.8 us
  transfers between devices with their start and end apart: 10, of which 9 were waited for; matrix products, arithmetic and copies ran while one was open for 14% of the time, Pallas kernels for 0%

profile of v1, /device:TPU:0, one launch (start us, length us, event | category | flops | bytes accessed | tf_op | source)
XLA Modules:
  0.0 856.3 jit_solution(6613501942638528276)
XLA Ops:
  7.2 5.4 stack.88
  12.6 7.6 all-to-all-start
  21.6 150.2 %all-to-all-done = bf16[16,128,2048]{2,1,0:T(8,128)(2,1)} async-done(((bf16[16,128,2048]{2,1,0:T(8,128)(2,1)}), bf16[16,128,2048]{2,1,0:T(8,128)(2,1)}, u32[]{:S(2)}, u32[]{:S(2)}) %all-to-all-start) | async-done | bytes 8388640 | tf_op jit(solution)/shard_map/all_to_all | solution.py:108
  171.8 4.6 convolution_convert_fusion.1
  176.5 13.0 %collective-permute-start = (bf16[3,3,2048]{2,1,0:T(4,128)(2,1)S(1)}, bf16[3,3,2048]{2,1,0:T(4,128)(2,1)S(1)}, u32[]{:S(2)}, u32[]{:S(2)}) collective-permute-start(bf16[3,3,2048]{2,1,0:T(4,128)(2,1)S(1)} %pad_maximum_fusion.5), channel_id=1, source_target_pairs={{0,2},{2,4},{4,6},{6,8},{8,10},{10,12},{12,14},{1,3},{3,5},{5,7},{... | collective-permute-start | bytes 110600 | tf_op jit(solution)/shard_map/ppermute | solution.py:13
  199.9 38.0 %all-reduce = f32[128]{0:T(128)S(1)} all-reduce(f32[128]{0:T(128)S(1)} %dynamic-update-slice), channel_id=2, replica_groups=mesh['parts'=2,'seq'=8,'rep'=2,'head'=1] {'seq'}, use_global_device_ids=true, to_apply=%add | all-reduce | flops 128 | bytes 1024
  244.0 2.4 fusion.19
  246.4 53.7 %all-gather.14.cloned.1.call-done = f32[128,128,128]{2,1,0:T(8,128)} async-done(((f32[16,128,128]{2,1,0:T(8,128)}), f32[128,128,128]{2,1,0:T(8,128)}) %all-gather.14.cloned.1.call-update) | async-done | bytes 8388624 | tf_op jit(solution)/shard_map/all_gather | solution.py:20
  301.2 2.6 fusion.18
  303.8 78.4 %all-gather.16.cloned.1.call-done = f32[128,128,128]{2,1,0:T(8,128)} async-done(((f32[16,128,128]{2,1,0:T(8,128)}), f32[128,128,128]{2,1,0:T(8,128)}) %all-gather.16.cloned.1.call-update) | async-done | bytes 8388624 | tf_op jit(solution)/shard_map/all_gather | solution.py:20
  383.3 18.8 %while.57 = (s32[]{:T(128)}, f32[16,128,128]{2,1,0:T(8,128)}, s32[]{:T(128)}, f32[8,16]{1,0:T(8,128)S(1)}, f32[8,16,128,128]{3,2,1,0:T(8,128)}, /*index=5*/s32[]{:T(128)}, s32[]{:T(128)}, s32[]{:T(128)}, s32[]{:T(128)}) while((s32[]{:T(128)}, f32[16,128,128]{2,1,0:T(8,128)}, s32[]{:T(128)}, f32[8,16]{1,0:T(8,128)S(1)}, ...), condition=%wide.region_4.5_spmd, body=%wide.region_3.4_spmd.sunk | while | flops 524294 | bytes 3146067 | solution.py:29
  383.3 2.7 bitcast_add_fusion.5
  386.0 2.7 bitcast_add_fusion.5
  388.6 2.7 bitcast_add_fusion.5
  391.3 2.7 bitcast_add_fusion.5
  394.0 2.7 bitcast_add_fusion.5
  396.7 2.7 bitcast_add_fusion.5
  399.4 2.7 bitcast_add_fusion.5
  412.1 14.6 %all-reduce.1 = bf16[128]{0:T(256)(128)(2,1)S(1)} all-reduce(bf16[128]{0:T(256)(128)(2,1)S(1)} %dynamic-update-slice.1), channel_id=7, replica_groups=mesh['parts'=2,'seq'=8,'rep'=2,'head'=1] {'seq'}, use_global_device_ids=true, to_apply=%add.1 | all-reduce | flops 128 | bytes 512
  434.9 19.0 %all-gather.18.cloned.1.call-done = bf16[128,128,128]{2,1,0:T(8,128)(2,1)} async-done(((bf16[16,128,128]{2,1,0:T(8,128)(2,1)}), bf16[128,128,128]{2,1,0:T(8,128)(2,1)}) %all-gather.18.cloned.1.call-update) | async-done | bytes 4194320 | tf_op jit(solution)/shard_map/all_gather | solution.py:35
  453.9 20.0 %while.58 = (s32[]{:T(128)}, f32[16,128,128]{2,1,0:T(8,128)}, s32[]{:T(128)}, bf16[8,16]{1,0:T(8,128)(2,1)S(1)}, bf16[8,16,128,128]{3,2,1,0:T(8,128)(2,1)}, /*index=5*/s32[]{:T(128)}, s32[]{:T(128)}) while((s32[]{:T(128)}, f32[16,128,128]{2,1,0:T(8,128)}, s32[]{:T(128)}, bf16[8,16]{1,0:T(8,128)(2,1)S(1)}, ...), condition=%wide.region_8.9_spmd.clone, body=%wide.region_7.8_spmd.clone.sunk | while | flops 1310740 | bytes 2621705 | solution.py:53
  456.2 2.5 fusion.119
  458.7 2.5 fusion.119
  461.2 2.6 fusion.119
  463.9 2.5 fusion.119
  466.4 2.5 fusion.119
  468.9 2.5 fusion.119
  471.4 2.5 fusion.119
  474.0 2.8 fusion.10
  476.8 24.4 %all-gather.20.cloned.1.call-done = bf16[128,128,128]{2,1,0:T(8,128)(2,1)} async-done(((bf16[16,128,128]{2,1,0:T(8,128)(2,1)}), bf16[128,128,128]{2,1,0:T(8,128)(2,1)}) %all-gather.20.cloned.1.call-update) | async-done | bytes 4194320 | tf_op jit(solution)/shard_map/all_gather | solution.py:35
  501.2 20.8 %while.59 = (s32[]{:T(128)}, f32[16,128,128]{2,1,0:T(8,128)}, s32[]{:T(128)}, bf16[8,16]{1,0:T(8,128)(2,1)S(1)}, bf16[8,16,128,128]{3,2,1,0:T(8,128)(2,1)}, /*index=5*/s32[]{:T(128)}, s32[]{:T(128)}, s32[]{:T(128)}, s32[]{:T(128)}) while((s32[]{:T(128)}, f32[16,128,128]{2,1,0:T(8,128)}, s32[]{:T(128)}, ...), condition=%wide.region_10.11_spmd.clone, body=%wide.region_9.10_spmd.clone.sunk | while | flops 1310744 | bytes 2621767 | solution.py:53
  503.5 2.6 fusion.120
  506.1 2.6 fusion.120
  508.7 2.7 fusion.120
  511.4 2.6 fusion.120
  514.1 2.6 fusion.120
  516.7 2.6 fusion.120
  519.3 2.6 fusion.120
  536.2 2.6 copy.157
  538.9 3.8 multiply_reduce_fusion.3
  542.7 8.1 multiply_bitcast_fusion
  555.4 2.7 copy.126
  558.0 4.1 multiply_reduce_fusion.11
  564.7 11.6 %all-gather.12.cloned.1.call-done = bf16[2048,2048]{1,0:T(8,128)(2,1)} async-done(((bf16[128,2048]{1,0:T(8,128)(2,1)}), bf16[2048,2048]{1,0:T(8,128)(2,1)}) %all-gather.12.cloned.1.call-update) | async-done | bytes 8388624 | tf_op jit(solution)/shard_map/all_gather | solution.py:258
  576.3 7.1 fusion.2
  583.4 172.6 %reduce-scatter.2.cloned.1.call-done = f32[128,2048]{0,1:T(8,128)} async-done(((f32[2048,2048]{0,1:T(8,128)}), f32[128,2048]{0,1:T(8,128)}) %reduce-scatter.2.cloned.1.call-update) | async-done | bytes 1048592 | tf_op jit(solution)/shard_map/reduce_scatter | solution.py:266
  756.0 2.5 copy.138
  758.6 89.3 %all-reduce.4.cloned.1.call-done = f32[3,4,2048]{2,1,0:T(4,128)} async-done(((f32[3,4,2048]{2,1,0:T(4,128)}), f32[3,4,2048]{2,1,0:T(4,128)}) %all-reduce.4.cloned.1.call-update) | async-done | bytes 98320 | tf_op jit(solution)/shard_map/psum | solution.py:255
  (159 shorter events, 65.0 us)
Async XLA Ops:
  7.2 164.7 %copy-start = (bf16[1,128,2048]{2,1,0:T(8,128)(2,1)S(1)}, bf16[1,128,2048]{2,1,0:T(8,128)(2,1)}, u32[]{:S(2)}) copy-start(bf16[1,128,2048]{2,1,0:T(8,128)(2,1)} %param.15) | copy-start | bytes 1572868
  12.6 8.4 copy-start.22
  12.6 8.4 copy-start.25
  12.6 8.9 %copy-start.24 = (f32[3,4,2048]{2,1,0:T(4,128)S(1)}, f32[3,4,2048]{2,1,0:T(4,128)}, u32[]{:S(2)}) copy-start(f32[3,4,2048]{2,1,0:T(4,128)} %param.20) | copy-start | bytes 294916
  12.6 159.2 %all-to-all-start = ((bf16[16,128,2048]{2,1,0:T(8,128)(2,1)}), bf16[16,128,2048]{2,1,0:T(8,128)(2,1)}, u32[]{:S(2)}, u32[]{:S(2)}) async-start(bf16[16,128,2048]{2,1,0:T(8,128)(2,1)} %stack.88), calls=%async_computation | async-start | bytes 16777216 | tf_op jit(solution)/shard_map/all_to_all | solution.py:108
  20.1 280.0 %all-gather.14.cloned.1.call-start = ((), (), s32[]{:S(2)}) async-start(), calls=%async_computation.5 | async-start | bytes 9437184 | tf_op jit(solution)/shard_map/all_gather | solution.py:20
  176.5 13.8 %collective-permute-start = (bf16[3,3,2048]{2,1,0:T(4,128)(2,1)S(1)}, bf16[3,3,2048]{2,1,0:T(4,128)(2,1)S(1)}, u32[]{:S(2)}, u32[]{:S(2)}) collective-permute-start(bf16[3,3,2048]{2,1,0:T(4,128)(2,1)S(1)} %pad_maximum_fusion.5), channel_id=1, source_target_pairs={{0,2},{2,4},{4,6},{6,8},{8,10},{10,12},{12,14},{1,3},{3,5},{5,7},{... | collective-permute-start | bytes 110600 | tf_op jit(solution)/shard_map/ppermute | solution.py:13
  193.3 2.7 copy-start.9
  193.8 0.8 copy-start.12
  195.9 186.2 %all-gather.16.cloned.1.call-start = ((), (), s32[]{:S(2)}) async-start(), calls=%async_computation.6 | async-start | bytes 9437184 | tf_op jit(solution)/shard_map/all_gather | solution.py:20
  196.0 2.4 copy-start.26
  198.3 41.9 %copy-start.23 = (bf16[1,128,2048]{2,1,0:T(8,128)(2,1)S(1)}, bf16[1,128,2048]{2,1,0:T(8,128)(2,1)}, u32[]{:S(2)}) copy-start(bf16[1,128,2048]{2,1,0:T(8,128)(2,1)} %param.17) | copy-start | bytes 1572868
  198.3 255.6 %all-gather.18.cloned.1.call-start = ((), (), s32[]{:S(2)}) async-start(), calls=%async_computation.7 | async-start | bytes 4718592 | tf_op jit(solution)/shard_map/all_gather | solution.py:35
  240.3 1.1 copy-start.1
  402.1 2.0 copy-start.13
  402.1 2.0 copy-start.20
  404.1 1.2 copy-start.14
  406.6 0.8 copy-start.6
  408.7 92.5 %all-gather.20.cloned.1.call-start = ((), (), s32[]{:S(2)}) async-start(), calls=%async_computation.8 | async-start | bytes 4718592 | tf_op jit(solution)/shard_map/all_gather | solution.py:35
  411.0 165.3 %all-gather.12.cloned.1.call-start = ((), (), s32[]{:S(2)}) async-start(), calls=%async_computation.2 | async-start | bytes 8912896 | tf_op jit(solution)/shard_map/all_gather | solution.py:258
  411.6 344.4 %reduce-scatter.2.cloned.1.call-start = ((), (), s32[]{:S(2)}) async-start(), calls=%async_computation.3 | async-start | bytes 17825792 | tf_op jit(solution)/shard_map/reduce_scatter | solution.py:266
  426.8 1.9 copy-start.4
  426.8 1.9 copy-start.7
  428.7 1.8 copy-start.17
  428.7 1.4 copy-start.3
  430.2 1.0 copy-start.10
  521.9 2.3 copy-start.18
  525.6 2.1 copy-start.11
  527.7 1.7 copy-start.5
  529.4 1.0 copy-start.8
  529.4 1.2 copy-start.21
  532.0 2.1 copy-start.19
  534.9 3.9 collective-permute-start.1
  550.8 1.2 copy-start.15
  550.8 297.1 %all-reduce.4.cloned.1.call-start = ((), (), s32[]{:S(2)}) async-start(), calls=%async_computation.4 | async-start | bytes 196608 | tf_op jit(solution)/shard_map/psum | solution.py:255
  555.4 2.7 copy-start.2
  558.0 4.1 copy-start.16
Sparse Core Ops, SparseCore 0:
  196.0 104.0 all-gather.13
  301.7 80.4 all-gather.15
  408.8 45.1 all-gather.17
  455.4 45.7 all-gather.19
  503.2 73.0 all-gather.11
  580.3 175.6 reduce-scatter.1
  760.0 87.8 all-reduce.3
